TPU v7x, 32 devices: a whole 2x2x4 slice. The times are simulated.
32 devices in a mesh: row: 8 (over y, x, core), col: 4 (over z).
Axes of the slice: x: 2, y: 2, z: 4, core: 2. Of those that a mesh axis runs over, the one named last changes fastest.
Arguments:
- node_features: bfloat16 [8192, 128], P(('row', 'col')), may hold values from -6 to 6
- tile_values: bfloat16 [8, 4, 384, 128, 128], P('row', 'col'), may hold values from -0.078125 to 0.078125
- tile_rows: int32 [8, 4, 384], P('row', 'col'), may hold values from 0 to 7
- tile_cols: int32 [8, 4, 384], P('row', 'col'), may hold values from 0 to 15
- tile_count: int32 [8, 4], P('row', 'col'), may hold values from 48 to 384, as said below
- labels: int32 [8192], P(('row', 'col')), may hold values from 0 to 46
- train_mask: int32 [8192], P(('row', 'col')), may hold values from 0 to 1, as said below
- hidden_weight: bfloat16 [128, 256], replicated, may hold values from -0.5 to 0.5
- hidden_bias: float32 [256], replicated, may hold values from -3 to 3
- class_weight: bfloat16 [256, 47], replicated, may hold values from -3.59375 to 3.59375
- class_bias: float32 [47], replicated, may hold values from -4 to 4
Outputs:
- hidden: bfloat16 [8192, 256], P(('row', 'col'))
- logits: float32 [47, 8192], P(None, ('row', 'col'))
- mean_loss: float32 [], replicated
- hidden_weight_grad: float32 [128, 256], replicated
- hidden_bias_grad: float32 [256], replicated
- class_weight_grad: float32 [256, 47], replicated
- class_bias_grad: float32 [47], replicated
Inputs may be any that keep to these rules, and one draw needn't show every extreme that they name: Slots s >= tile_count of a block are not part of it; some block has all 384 slots live. `train_mask`: at least one node is a training node.
All inputs are finite; a program needn't handle non-finite values.
Results may differ from a plain program's by a relative error of at most 0.025.
Values may be sent and summed in bfloat16 or wider, within the bound.
No kernel may reach another device: no remote copies, remote signals or barrier semaphores. Data moves between devices by JAX's collectives and lax.ppermute only.
A program may use at most 128 MiB of HBM per device.

v0:
```python
import math
import jax
import jax.numpy as jnp
from jax import lax
from jax.sharding import PartitionSpec as P


def tile_product(values, source_tile, target_tile, live_slots, source, out_tiles, transpose):
    feature_width = source.shape[1]
    wide_source = source.dtype == jnp.float32
    tiled = source.reshape(-1, 128, feature_width)
    slot_count = values.shape[0]
    group_size = math.gcd(slot_count, 32)
    rounds = slot_count // group_size
    grouped = (
        values.reshape(rounds, group_size, 128, 128),
        source_tile.reshape(rounds, group_size),
        target_tile.reshape(rounds, group_size),
        live_slots.reshape(rounds, group_size),
    )
    pattern = "gji,gjf->gif" if transpose else "gij,gjf->gif"
    targets = jnp.arange(out_tiles, dtype=jnp.int32)

    def one_group(totals, item):
        tiles_in, from_tile, to_tile, alive = item
        pieces = tiled[from_tile]
        if wide_source:
            product = jnp.einsum(
                pattern, tiles_in.astype(jnp.float32), pieces, precision=lax.Precision.HIGHEST
            )
        else:
            product = jnp.einsum(pattern, tiles_in, pieces, preferred_element_type=jnp.float32)
        placing = (targets[:, None] == to_tile[None, :]).astype(jnp.float32) * alive[None, :]
        placed = jnp.einsum("og,gif->oif", placing, product, precision=lax.Precision.HIGHEST)
        return (totals + placed, None)

    start = jnp.zeros((out_tiles, 128, feature_width), jnp.float32)
    totals, _ = lax.scan(one_group, start, grouped)
    return totals.reshape(out_tiles * 128, feature_width)


def pre_activation(aggregated, hidden_weight, hidden_bias):
    return jnp.dot(aggregated, hidden_weight, preferred_element_type=jnp.float32) + hidden_bias


def on_device(
    node_features,
    tile_values,
    tile_rows,
    tile_cols,
    tile_count,
    labels,
    train_mask,
    hidden_weight,
    hidden_bias,
    class_weight,
    class_bias,
):
    nodes_here = node_features.shape[0]
    values = tile_values[0, 0]
    rows_here = tile_rows[0, 0]
    cols_here = tile_cols[0, 0]
    live_slots = (jnp.arange(values.shape[0]) < tile_count[0, 0]).astype(jnp.float32)
    block_rows = lax.axis_size("col") * nodes_here // 128
    block_cols = lax.axis_size("row") * nodes_here // 128
    class_weight_wide = class_weight.astype(jnp.float32)
    gathered = lax.all_gather(node_features, "row", axis=0, tiled=True)
    first_term = tile_product(values, cols_here, rows_here, live_slots, gathered, block_rows, False)
    first_agg = lax.psum_scatter(
        first_term.astype(jnp.bfloat16), "col", scatter_dimension=0, tiled=True
    )
    hidden_pre = pre_activation(first_agg, hidden_weight, hidden_bias)
    hidden = jax.nn.silu(hidden_pre).astype(jnp.bfloat16)
    hidden_column = lax.all_gather(hidden, "row", axis=0, tiled=True)
    second_term = tile_product(
        values, cols_here, rows_here, live_slots, hidden_column, block_rows, False
    )
    second_agg = lax.psum_scatter(
        second_term.astype(jnp.bfloat16), "col", scatter_dimension=0, tiled=True
    ).astype(jnp.float32)
    logits = (
        jnp.einsum("hk,nh->kn", class_weight_wide, second_agg, precision=lax.Precision.HIGHEST)
        + class_bias[:, None]
    )
    top = jnp.max(logits, axis=0)
    log_total = top + jnp.log(jnp.sum(jnp.exp(logits - top[None, :]), axis=0))
    onehot = (jnp.arange(logits.shape[0])[:, None] == labels[None, :]).astype(jnp.float32)
    cross_entropy = log_total - jnp.sum(onehot * logits, axis=0)
    weights = train_mask.astype(jnp.float32)
    count, loss_total = lax.psum(
        (jnp.sum(weights), jnp.sum(weights * cross_entropy)), ("row", "col")
    )
    mean_loss = loss_total / count
    class_grad = (jnp.exp(logits - log_total[None, :]) - onehot) * (weights / count)[None, :]
    class_bias_part = jnp.sum(class_grad, axis=1)
    class_weight_part = jnp.einsum(
        "nh,kn->hk", second_agg, class_grad, precision=lax.Precision.HIGHEST
    )
    agg_grad = jnp.einsum(
        "kn,hk->nh", class_grad, class_weight_wide, precision=lax.Precision.HIGHEST
    )
    grad_block = lax.all_gather(agg_grad.astype(jnp.bfloat16), "col", axis=0, tiled=True).astype(
        agg_grad.dtype
    )
    back_term = tile_product(values, rows_here, cols_here, live_slots, grad_block, block_cols, True)
    hidden_grad = lax.psum_scatter(
        back_term.astype(jnp.bfloat16), "row", scatter_dimension=0, tiled=True
    ).astype(jnp.float32)
    sigma = jax.nn.sigmoid(hidden_pre)
    pre_grad = hidden_grad * sigma * (1.0 + hidden_pre * (1.0 - sigma))
    hidden_weight_part = jnp.einsum(
        "nf,nh->fh", first_agg.astype(jnp.float32), pre_grad, precision=lax.Precision.HIGHEST
    )
    hidden_bias_part = jnp.sum(pre_grad, axis=0)
    hidden_weight_grad, hidden_bias_grad, class_weight_grad, class_bias_grad = lax.psum(
        (hidden_weight_part, hidden_bias_part, class_weight_part, class_bias_part), ("row", "col")
    )
    return (
        hidden,
        logits,
        mean_loss,
        hidden_weight_grad,
        hidden_bias_grad,
        class_weight_grad,
        class_bias_grad,
    )


def solution(mesh):
    in_specs = (
        P(("row", "col"), None),
        P("row", "col", None, None, None),
        P("row", "col", None),
        P("row", "col", None),
        P("row", "col"),
        P(("row", "col")),
        P(("row", "col")),
        P(),
        P(),
        P(),
        P(),
    )
    out_specs = (P(("row", "col"), None), P(None, ("row", "col")), P(), P(), P(), P(), P())
    return jax.shard_map(
        on_device, mesh=mesh, in_specs=in_specs, out_specs=out_specs, check_vma=False
    )
```

profile of v0, /device:TPU:0, one launch (start us, length us, event | category | flops | bytes accessed | tf_op | source)
XLA Modules:
  0.0 682.8 jit_solution(6361040760359997796)
XLA Ops:
  10.6 11.6 %all_gather.9 = bf16[2048,128]{1,0:T(8,128)(2,1)S(1)} all-gather(bf16[256,128]{1,0:T(8,128)(2,1)} %param.17), channel_id=1, replica_groups=mesh['row'=8,'col'=4] {'row'}, dimensions={0}, use_global_device_ids=true | all-gather | bytes 589824 | tf_op jit(solution)/shard_map/all_gather | solution.py:67
  22.3 74.5 %while.33 = (s32[]{:T(128)}, f32[8,128,128]{2,0,1:T(8,128)S(1)}, s32[12,32]{1,0:T(8,128)}, f32[12,32]{1,0:T(8,128)}, bf16[12,32,128,128]{3,2,1,0:T(8,128)(2,1)},...) while((s32[]{:T(128)}, f32[8,128,128]{2,0,1:T(8,128)S(1)}, ...), condition=%wide.region_1.2_spmd.clone, body=%wide.region_0.1_spmd.clone.sunk | while | flops 184813152 | bytes 9442687 | solution.py:38
  97.6 20.4 %reduce-scatter.4.cloned.1.call-done = bf16[256,128]{1,0:T(8,128)(2,1)} async-done(((bf16[1024,128]{1,0:T(8,128)(2,1)}), bf16[256,128]{1,0:T(8,128)(2,1)}) %reduce-scatter.4.cloned.1.call-update) | async-done | bytes 65552 | tf_op jit(solution)/shard_map/reduce_scatter | solution.py:69
  119.8 22.3 %all-gather.2.cloned.1.call-done = bf16[2048,256]{1,0:T(8,128)(2,1)} async-done(((bf16[256,256]{1,0:T(8,128)(2,1)}), bf16[2048,256]{1,0:T(8,128)(2,1)}) %all-gather.2.cloned.1.call-update) | async-done | bytes 1048592 | tf_op jit(solution)/shard_map/all_gather | solution.py:74
  142.1 120.3 %while.34 = (s32[]{:T(128)}, f32[8,128,256]{2,0,1:T(8,128)S(1)}, s32[12,32]{1,0:T(8,128)}, f32[12,32]{1,0:T(8,128)}, bf16[12,32,128,128]{3,2,1,0:T(8,128)(2,1)},...) while((s32[]{:T(128)}, f32[8,128,256]{2,0,1:T(8,128)S(1)}, ...), condition=%wide.region_4.5_spmd.clone, body=%wide.region_3.4_spmd.clone.sunk | while | flops 369624672 | bytes 17831296 | solution.py:38
  264.2 39.5 %psum.43 = f32[]{:T(128)} all-reduce(f32[]{:T(128)} %convert_reduce_fusion), channel_id=1, replica_groups=mesh['row'=8,'col'=4] {'row','col'}, use_global_device_ids=true, to_apply=%region_12.13 | all-reduce | flops 1 | bytes 8 | tf_op jit(solution)/shard_map/psum | solution.py:90
  306.6 15.6 %all_gather.11 = bf16[1024,256]{1,0:T(8,128)(2,1)S(1)} all-gather(bf16[256,256]{1,0:T(8,128)(2,1)S(1)} %convolution_convert_fusion), channel_id=1, replica_groups=mesh['row'=8,'col'=4] {'col'}, dimensions={0}, use_global_device_ids=true | all-gather | bytes 655360 | tf_op jit(solution)/shard_map/all_gather | solution.py:102
  322.3 181.8 %while.35 = (s32[]{:T(128)}, f32[16,128,256]{2,0,1:T(8,128)S(1)}, s32[12,32]{1,0:T(8,128)}, f32[12,32]{1,0:T(8,128)}, bf16[12,32,128,128]{3,2,1,0:T(8,128)(2,1)}...) while((s32[]{:T(128)}, f32[16,128,256]{2,0,1:T(8,128)S(1)}, ...), condition=%wide.region_14.15_spmd.clone, body=%wide.region_13.14_spmd.clone.sunk | while | flops 1812990080 | bytes 26219900 | solution.py:38
  327.2 4.9 fusion.128
  332.1 5.4 select_add_fusion.2
  347.2 5.4 select_add_fusion.2
  362.3 5.4 select_add_fusion.2
  377.5 5.4 select_add_fusion.2
  392.6 5.4 select_add_fusion.2
  407.8 5.4 select_add_fusion.2
  422.9 5.4 select_add_fusion.2
  438.1 5.4 select_add_fusion.2
  453.2 5.4 select_add_fusion.2
  468.4 5.4 select_add_fusion.2
  483.5 5.4 select_add_fusion.2
  498.7 5.4 select_add_fusion.2
  506.1 37.0 %reduce-scatter.8.cloned.1.call-done = bf16[256,256]{1,0:T(8,128)(2,1)} async-done(((bf16[2048,256]{1,0:T(8,128)(2,1)}), bf16[256,256]{1,0:T(8,128)(2,1)}) %reduce-scatter.8.cloned.1.call-update) | async-done | bytes 131088 | tf_op jit(solution)/shard_map/reduce_scatter | solution.py:106
  545.7 40.3 %all-reduce = (f32[]{:T(128)}, f32[256]{0:T(256)}, f32[256,47]{0,1:T(8,128)}, f32[47]{0:T(128)}) all-reduce(f32[]{:T(128)} %multiply_reduce_fusion, f32[256]{0:T(256)S(1)} %get-tuple-element.262, f32[256,47]{0,1:T(8,128)S(1)} %fusion.63, f32[47]{0:T(128)S(1)} %get-tuple-element.214), channel_id=1, replica_groups=mesh['row'=8,'col'=4] {'row','col'}, use_global_device_ids=true, to_apply=%region_10.11 | all-reduce | flops 12336 | bytes 98688 | tf_op jit(solution)/shard_map/psum | solution.py:90
  587.2 86.4 %all-reduce.3.cloned.1.call-done = f32[128,256]{1,0:T(8,128)} async-done(((f32[128,256]{1,0:T(8,128)}), f32[128,256]{1,0:T(8,128)}) %all-reduce.3.cloned.1.call-update) | async-done | bytes 131088 | tf_op jit(solution)/shard_map/psum | solution.py:115
  (296 shorter events, 321.4 us)
Async XLA Ops:
  7.2 110.8 %copy-start = (bf16[128,256]{1,0:T(8,128)(2,1)S(1)}, bf16[128,256]{1,0:T(8,128)(2,1)}, u32[]{:S(2)}) copy-start(bf16[128,256]{1,0:T(8,128)(2,1)} %param.24) | copy-start | bytes 196612
  7.2 110.8 %reduce-scatter.4.cloned.1.call-start = ((), (), s32[]{:S(2)}) async-start(), calls=%async_computation.3 | async-start | bytes 327680 | tf_op jit(solution)/shard_map/reduce_scatter | solution.py:69
  22.3 95.7 %copy-start.9 = (f32[256]{0:T(256)S(1)}, f32[256]{0:T(256)}, u32[]{:S(2)}) copy-start(f32[256]{0:T(256)} %param.25) | copy-start | bytes 3076
  97.6 44.5 %all-gather.2.cloned.1.call-start = ((), (), s32[]{:S(2)}) async-start(), calls=%async_computation.4 | async-start | bytes 1179648 | tf_op jit(solution)/shard_map/all_gather | solution.py:74
  119.7 184.7 %reduce-scatter.6.cloned.1.call-start = ((), (), s32[]{:S(2)}) async-start(), calls=%async_computation.5 | async-start | bytes 655360 | tf_op jit(solution)/shard_map/reduce_scatter | solution.py:78
  142.1 121.5 %copy-start.7 = (s32[256]{0:T(256)S(1)}, s32[256]{0:T(256)}, u32[]{:S(2)}) copy-start(s32[256]{0:T(256)} %param.23) | copy-start | bytes 3076
  142.1 162.3 %copy-start.3 = (bf16[256,47]{0,1:T(8,128)(2,1)S(1)}, bf16[256,47]{0,1:T(8,128)(2,1)}, u32[]{:S(2)}) copy-start(bf16[256,47]{0,1:T(8,128)(2,1)} %param.26) | copy-start | bytes 72196
  262.4 41.3 %copy-start.6 = (s32[12,32]{1,0:T(8,128)}, s32[12,32]{1,0:T(8,128)S(1)}, u32[]{:S(2)}) copy-start(s32[12,32]{1,0:T(8,128)S(1)} %get-tuple-element.508) | copy-start | bytes 4612
  263.5 279.6 %reduce-scatter.8.cloned.1.call-start = ((), (), s32[]{:S(2)}) async-start(), calls=%async_computation.6 | async-start | bytes 1179648 | tf_op jit(solution)/shard_map/reduce_scatter | solution.py:106
  305.5 200.3 %copy-start.1 = (f32[256,47]{0,1:T(8,128)}, f32[256,47]{0,1:T(8,128)S(1)}, u32[]{:S(2)}) copy-start(f32[256,47]{0,1:T(8,128)S(1)} %get-tuple-element.267) | copy-start | bytes 144388
  504.1 1.6 copy-start.5
  504.1 1.7 copy-start.2
  504.1 40.0 %copy-start.4 = (bf16[256,128]{1,0:T(8,128)(2,1)S(1)}, bf16[256,128]{1,0:T(8,128)(2,1)}, u32[]{:S(2)}) copy-start(bf16[256,128]{1,0:T(8,128)(2,1)} %reduce-scatter.4.cloned.1.call-done) | copy-start | bytes 196612
  504.1 40.9 %copy-start.8 = (s32[256]{0:T(256)S(1)}, s32[256]{0:T(256)}, u32[]{:S(2)}) copy-start(s32[256]{0:T(256)} %param.23) | copy-start | bytes 3076
  505.7 167.9 %all-reduce.3.cloned.1.call-start = ((), (), s32[]{:S(2)}) async-start(), calls=%async_computation.7 | async-start | bytes 262144 | tf_op jit(solution)/shard_map/psum | solution.py:115
Sparse Core Ops, SparseCore 0:
  97.7 20.2 reduce-scatter.3
  120.5 21.5 all-gather.1
  263.6 21.8 reduce-scatter.5
  505.8 37.2 reduce-scatter.7
  549.0 124.5 all-reduce.2
where the time goes:
time: 688 us; the launch traced here: 683 us
  matrix products  257 us (37%)
  waiting for transfers between devices  166 us (24%)
  local copies, waits for them, and re-layouts  120 us (17%)
  blocking collectives  107 us (16%)
  between operations  17 us (2%)
  other arithmetic  14.1 us (2%)
    dot_general x36, matrix products, one_group(): jnp.einsum('og,gif->oif', placing, product, precision=lax.Precision.HIGHEST)  150 us
    psum x1, waiting for transfers between devices, on_device(): lax.psum((hidden_weight_part, hidden_bias_part, class_weight_part, class_...  86.4 us
    psum x2, blocking collectives, on_device(): lax.psum((jnp.sum(weights), jnp.sum(weights * cross_entropy)), ('row', 'c...  79.8 us
    gather x36, local copies, waits for them, and re-layouts, one_group(): pieces = tiled[from_tile]  64.8 us
    dot_general x12, matrix products, one_group(): jnp.einsum(pattern, tiles_in.astype(jnp.float32), pieces, precision=lax.P...  58.6 us
    dot_general x24, matrix products, one_group(): jnp.einsum(pattern, tiles_in, pieces, preferred_element_type=jnp.float32)  43 us
    reduce_scatter x1, waiting for transfers between devices, on_device(): lax.psum_scatter(back_term.astype(jnp.bfloat16), 'row', scatter_dimension...  37 us
    mul x36, local copies, waits for them, and re-layouts, one_group(): (targets[:, None] == to_tile[None, :]).astype(jnp.float32) * alive[None, :]  25.1 us
  transfers between devices with their start and end apart: 5, of which 4 were waited for; matrix products, arithmetic and copies ran while one was open for 0% of the time, Pallas kernels for 0%

commit v1 on v0

--- a/solution.py
+++ b/solution.py
@@ -88,7 +88,7 @@
     cross_entropy = log_total - jnp.sum(onehot * logits, axis=0)
     weights = train_mask.astype(jnp.float32)
     count, loss_total = lax.psum(
-        (jnp.sum(weights), jnp.sum(weights * cross_entropy)), ("row", "col")
+        lax.psum((jnp.sum(weights), jnp.sum(weights * cross_entropy)), "col"), "row"
     )
     mean_loss = loss_total / count
     class_grad = (jnp.exp(logits - log_total[None, :]) - onehot) * (weights / count)[None, :]

time: 688 us -> 761 us (1.11)
  matrix products: 257 us -> 367 us
  waiting for transfers between devices: 166 us -> 140 us
  local copies, waits for them, and re-layouts: 120 us -> 100 us
  blocking collectives: 107 us -> 117 us
    dot_general x36, matrix products: 150 us -> 214 us  [one_group(): jnp.einsum('og,gif->oif', placing, product, precision=lax.Precision.HIGHEST)]
    dot_general x12, matrix products: 58.6 us -> 82.1 us  [one_group(): jnp.einsum(pattern, tiles_in.astype(jnp.float32), pieces, precision=lax.P...]
    dot_general x24, matrix products: 43 us -> 66.1 us  [one_group(): jnp.einsum(pattern, tiles_in, pieces, preferred_element_type=jnp.float32)]
    mul x36, local copies, waits for them, and re-layouts: 25.1 us -> 8.51 us  [one_group(): (targets[:, None] == to_tile[None, :]).astype(jnp.float32) * alive[None, :]]
    eq x36, local copies, waits for them, and re-layouts: 24.7 us -> 8.51 us  [one_group(): targets[:, None] == to_tile[None, :]]
    reduce_scatter x1, waiting for transfers between devices: 37 us -> 23.5 us  [on_device(): lax.psum_scatter(back_term.astype(jnp.bfloat16), 'row', scatter_dimension...]
    psum x1, waiting for transfers between devices: 86.4 us -> 73.7 us  [on_device(): lax.psum((hidden_weight_part, hidden_bias_part, class_weight_part, class_...]
    gather x36, local copies, waits for them, and re-layouts: 64.8 us -> 77.2 us  [one_group(): pieces = tiled[from_tile]]
where the time goes in v1:
time: 761 us; the launch traced here: 757 us
  matrix products  367 us (48%)
  waiting for transfers between devices  140 us (18%)
  blocking collectives  117 us (15%)
  local copies, waits for them, and re-layouts  100 us (13%)
  between operations  17.1 us (2%)
  other arithmetic  13.5 us (2%)
    dot_general x36, matrix products, one_group(): jnp.einsum('og,gif->oif', placing, product, precision=lax.Precision.HIGHEST)  214 us
    dot_general x12, matrix products, one_group(): jnp.einsum(pattern, tiles_in.astype(jnp.float32), pieces, precision=lax.P...  82.1 us
    gather x36, local copies, waits for them, and re-layouts, one_group(): pieces = tiled[from_tile]  77.2 us
    psum x1, waiting for transfers between devices, on_device(): lax.psum((hidden_weight_part, hidden_bias_part, class_weight_part, class_...  73.7 us
    dot_general x24, matrix products, one_group(): jnp.einsum(pattern, tiles_in, pieces, preferred_element_type=jnp.float32)  66.1 us
    psum x1, blocking collectives, on_device(): lax.psum((hidden_weight_part, hidden_bias_part, class_weight_part, class_...  40.3 us
    psum x2, blocking collectives, on_device(): lax.psum(lax.psum((jnp.sum(weights), jnp.sum(weights * cross_entropy)), '...  25.3 us
    reduce_scatter x1, waiting for transfers between devices, on_device(): lax.psum_scatter(back_term.astype(jnp.bfloat16), 'row', scatter_dimension...  23.5 us
  transfers between devices with their start and end apart: 5, of which 4 were waited for; matrix products, arithmetic and copies ran while one was open for 0% of the time, Pallas kernels for 0%

profile of v1, /device:TPU:0, one launch (start us, length us, event | category | flops | bytes accessed | tf_op | source)
XLA Modules:
  0.0 757.0 jit_solution(6717866308189952142)
XLA Ops:
  9.5 13.2 %all_gather.9 = bf16[2048,128]{1,0:T(8,128)(2,1)} all-gather(bf16[256,128]{1,0:T(8,128)(2,1)} %param.17), channel_id=1, replica_groups=mesh['row'=8,'col'=4] {'row'}, dimensions={0}, use_global_device_ids=true | all-gather | bytes 589824 | tf_op jit(solution)/shard_map/all_gather | solution.py:67
  22.7 90.2 %while.33 = (s32[]{:T(128)}, f32[8,128,128]{2,0,1:T(8,128)}, s32[12,32]{1,0:T(8,128)S(1)}, f32[12,32]{1,0:T(8,128)S(1)}, bf16[12,32,128,128]{3,2,1,0:T(8,128)(2,...) while((s32[]{:T(128)}, f32[8,128,128]{2,0,1:T(8,128)}, ...), condition=%wide.region_1.2_spmd.clone, body=%wide.region_0.1_spmd.clone.sunk | while | flops 184813152 | bytes 9443187 | solution.py:38
  114.8 20.4 %reduce-scatter.4.cloned.1.call-done = bf16[256,128]{1,0:T(8,128)(2,1)} async-done(((bf16[1024,128]{1,0:T(8,128)(2,1)}), bf16[256,128]{1,0:T(8,128)(2,1)}) %reduce-scatter.4.cloned.1.call-update) | async-done | bytes 65552 | tf_op jit(solution)/shard_map/reduce_scatter | solution.py:69
  137.0 22.3 %all-gather.2.cloned.1.call-done = bf16[2048,256]{1,0:T(8,128)(2,1)} async-done(((bf16[256,256]{1,0:T(8,128)(2,1)}), bf16[2048,256]{1,0:T(8,128)(2,1)}) %all-gather.2.cloned.1.call-update) | async-done | bytes 1048592 | tf_op jit(solution)/shard_map/all_gather | solution.py:74
  159.3 151.7 %while.34 = (s32[]{:T(128)}, f32[8,128,256]{2,0,1:T(8,128)S(1)}, s32[12,32]{1,0:T(8,128)S(1)}, f32[12,32]{1,0:T(8,128)S(1)}, bf16[12,32,128,128]{3,2,1,0:T(8,128...) while((s32[]{:T(128)}, f32[8,128,256]{2,0,1:T(8,128)S(1)}, ...), condition=%wide.region_4.5_spmd.clone, body=%wide.region_3.4_spmd.clone.sunk | while | flops 369624672 | bytes 17831796 | solution.py:38
  312.8 12.6 %psum.58 = f32[]{:T(128)} all-reduce(f32[]{:T(128)} %convert_reduce_fusion), channel_id=1, replica_groups=mesh['row'=8,'col'=4] {'col'}, use_global_device_ids=true, to_apply=%region_13.14 | all-reduce | flops 1 | bytes 8 | tf_op jit(solution)/shard_map/psum | solution.py:91
  325.4 12.4 %psum.59 = f32[]{:T(128)} all-reduce(f32[]{:T(128)} %psum.58), channel_id=1, replica_groups=mesh['row'=8,'col'=4] {'row'}, use_global_device_ids=true, to_apply=%region_14.15 | all-reduce | flops 1 | bytes 8 | tf_op jit(solution)/shard_map/psum | solution.py:90
  340.7 16.3 %all_gather.11 = bf16[1024,256]{1,0:T(8,128)(2,1)S(1)} all-gather(bf16[256,256]{1,0:T(8,128)(2,1)S(1)} %convolution_convert_fusion), channel_id=1, replica_groups=mesh['row'=8,'col'=4] {'col'}, dimensions={0}, use_global_device_ids=true | all-gather | bytes 655360 | tf_op jit(solution)/shard_map/all_gather | solution.py:102
  357.2 224.9 %while.35 = (s32[]{:T(128)}, f32[16,128,256]{2,0,1:T(8,128)S(1)}, s32[12,32]{1,0:T(8,128)}, f32[12,32]{1,0:T(8,128)}, bf16[12,32,128,128]{3,2,1,0:T(8,128)(2,1)}...) while((s32[]{:T(128)}, f32[16,128,256]{2,0,1:T(8,128)S(1)}, ...), condition=%wide.region_16.17_spmd.clone, body=%wide.region_15.16_spmd.clone.sunk | while | flops 1812990080 | bytes 26220400 | solution.py:38
  368.8 7.1 select_add_fusion.2
  387.6 7.1 select_add_fusion.2
  406.3 7.1 select_add_fusion.2
  425.1 7.1 select_add_fusion.2
  443.8 7.1 select_add_fusion.2
  462.6 7.1 select_add_fusion.2
  481.3 7.1 select_add_fusion.2
  500.1 7.1 select_add_fusion.2
  518.8 7.1 select_add_fusion.2
  537.5 7.1 select_add_fusion.2
  584.5 9.3 %psum.56 = f32[]{:T(128)} all-reduce(f32[]{:T(128)} %multiply_reduce_fusion), channel_id=1, replica_groups=mesh['row'=8,'col'=4] {'col'}, use_global_device_ids=true, to_apply=%region_10.11 | all-reduce | flops 1 | bytes 8 | tf_op jit(solution)/shard_map/psum | solution.py:91
  593.7 23.5 %reduce-scatter.8.cloned.1.call-done = bf16[256,256]{1,0:T(8,128)(2,1)} async-done(((bf16[2048,256]{1,0:T(8,128)(2,1)}), bf16[256,256]{1,0:T(8,128)(2,1)}) %reduce-scatter.8.cloned.1.call-update) | async-done | bytes 131088 | tf_op jit(solution)/shard_map/reduce_scatter | solution.py:106
  619.5 12.9 %psum.57 = f32[]{:T(128)} all-reduce(f32[]{:T(128)} %psum.56), channel_id=1, replica_groups=mesh['row'=8,'col'=4] {'row'}, use_global_device_ids=true, to_apply=%region_11.12 | all-reduce | flops 1 | bytes 8 | tf_op jit(solution)/shard_map/psum | solution.py:90
  633.8 40.3 %all-reduce = (f32[256]{0:T(256)}, f32[256,47]{0,1:T(8,128)}, f32[47]{0:T(128)}) all-reduce(f32[256]{0:T(256)S(1)} %get-tuple-element.261, f32[256,47]{0,1:T(8,128)S(1)} %fusion.63, f32[47]{0:T(128)S(1)} %get-tuple-element.214), channel_id=1, replica_groups=mesh['row'=8,'col'=4] {'row','col'}, use_global_device_ids=true, to_apply=%region_20.21 | all-reduce | flops 12335 | bytes 98680 | tf_op jit(solution)/shard_map/psum | solution.py:115
  674.1 73.7 %all-reduce.3.cloned.1.call-done = f32[128,256]{1,0:T(8,128)} async-done(((f32[128,256]{1,0:T(8,128)}), f32[128,256]{1,0:T(8,128)}) %all-reduce.3.cloned.1.call-update) | async-done | bytes 131088 | tf_op jit(solution)/shard_map/psum | solution.py:115
  (303 shorter events, 411.0 us)
Async XLA Ops:
  7.2 128.0 %copy-start = (bf16[128,256]{1,0:T(8,128)(2,1)S(1)}, bf16[128,256]{1,0:T(8,128)(2,1)}, u32[]{:S(2)}) copy-start(bf16[128,256]{1,0:T(8,128)(2,1)} %param.24) | copy-start | bytes 196612
  7.2 128.0 %reduce-scatter.4.cloned.1.call-start = ((), (), s32[]{:S(2)}) async-start(), calls=%async_computation.3 | async-start | bytes 327680 | tf_op jit(solution)/shard_map/reduce_scatter | solution.py:69
  22.7 112.5 %copy-start.11 = (f32[256]{0:T(256)S(1)}, f32[256]{0:T(256)}, u32[]{:S(2)}) copy-start(f32[256]{0:T(256)} %param.25) | copy-start | bytes 3076
  114.8 44.5 %all-gather.2.cloned.1.call-start = ((), (), s32[]{:S(2)}) async-start(), calls=%async_computation.4 | async-start | bytes 1179648 | tf_op jit(solution)/shard_map/all_gather | solution.py:74
  136.9 201.6 %reduce-scatter.6.cloned.1.call-start = ((), (), s32[]{:S(2)}) async-start(), calls=%async_computation.5 | async-start | bytes 655360 | tf_op jit(solution)/shard_map/reduce_scatter | solution.py:78
  159.3 152.9 %copy-start.9 = (s32[256]{0:T(256)S(1)}, s32[256]{0:T(256)}, u32[]{:S(2)}) copy-start(s32[256]{0:T(256)} %param.23) | copy-start | bytes 3076
  159.3 179.2 %copy-start.3 = (bf16[256,47]{0,1:T(8,128)(2,1)S(1)}, bf16[256,47]{0,1:T(8,128)(2,1)}, u32[]{:S(2)}) copy-start(bf16[256,47]{0,1:T(8,128)(2,1)} %param.26) | copy-start | bytes 72196
  311.0 27.4 %copy-start.6 = (s32[12,32]{1,0:T(8,128)}, s32[12,32]{1,0:T(8,128)S(1)}, u32[]{:S(2)}) copy-start(s32[12,32]{1,0:T(8,128)S(1)} %get-tuple-element.507) | copy-start | bytes 4612
  311.0 27.4 %copy-start.7 = (s32[12,32]{1,0:T(8,128)}, s32[12,32]{1,0:T(8,128)S(1)}, u32[]{:S(2)}) copy-start(s32[12,32]{1,0:T(8,128)S(1)} %get-tuple-element.509) | copy-start | bytes 4612
  311.0 27.4 %copy-start.8 = (f32[12,32]{1,0:T(8,128)}, f32[12,32]{1,0:T(8,128)S(1)}, u32[]{:S(2)}) copy-start(f32[12,32]{1,0:T(8,128)S(1)} %get-tuple-element.511) | copy-start | bytes 4612
  312.2 305.1 %reduce-scatter.8.cloned.1.call-start = ((), (), s32[]{:S(2)}) async-start(), calls=%async_computation.6 | async-start | bytes 1179648 | tf_op jit(solution)/shard_map/reduce_scatter | solution.py:106
  339.6 279.6 %copy-start.1 = (f32[256,47]{0,1:T(8,128)}, f32[256,47]{0,1:T(8,128)S(1)}, u32[]{:S(2)}) copy-start(f32[256,47]{0,1:T(8,128)S(1)} %get-tuple-element.266) | copy-start | bytes 144388
  582.1 1.6 copy-start.5
  582.1 1.7 copy-start.10
  582.1 36.2 %copy-start.4 = (bf16[256,128]{1,0:T(8,128)(2,1)S(1)}, bf16[256,128]{1,0:T(8,128)(2,1)}, u32[]{:S(2)}) copy-start(bf16[256,128]{1,0:T(8,128)(2,1)} %reduce-scatter.4.cloned.1.call-done) | copy-start | bytes 196612
  582.1 37.1 %copy-start.2 = (bf16[256,256]{1,0:T(8,128)(2,1)S(1)}, bf16[256,256]{1,0:T(8,128)(2,1)}, u32[]{:S(2)}) copy-start(bf16[256,256]{1,0:T(8,128)(2,1)} %reduce-scatter.6.cloned.1.call-done) | copy-start | bytes 393220
  583.7 164.1 %all-reduce.3.cloned.1.call-start = ((), (), s32[]{:S(2)}) async-start(), calls=%async_computation.7 | async-start | bytes 262144 | tf_op jit(solution)/shard_map/psum | solution.py:115
Sparse Core Ops, SparseCore 0:
  114.9 20.2 reduce-scatter.3
  137.7 21.6 all-gather.1
  312.3 21.8 reduce-scatter.5
  583.8 33.4 reduce-scatter.7
  623.2 124.4 all-reduce.2
